TPU v7x, 512 devices: a whole 4x8x8 slice. The times are simulated.
512 devices in a mesh: fsdp: 32 (over z, y_hi), tensor: 16 (over x, y_lo, core).
Axes of the slice: x: 4, y: 8 (y_hi: 4, y_lo: 2; y = y_hi * 2 + y_lo), z: 8, core: 2. Of those that a mesh axis runs over, the one named last changes fastest.
Arguments:
- old_codes: bfloat16 [26624, 16384], P(('fsdp', 'tensor')), may hold values from -1 to 1
- old_scales: float32 [208, 128], replicated, may hold values from 0.003 to 0.03
- gate_pre: bfloat16 [2048, 26624], P('fsdp', 'tensor'), may hold values from -6 to 6
- up_pre: bfloat16 [2048, 26624], P('fsdp', 'tensor'), may hold values from -6 to 6
Outputs:
- mixed: bfloat16 [2048, 16384], P('tensor', 'fsdp')
- codes_t: bfloat16 [16384, 26624], P('fsdp', 'tensor')
- scales_t: float32 [128, 208], P('fsdp', 'tensor')
All inputs are finite; a program needn't handle non-finite values. Where the computation divides by a largest or mean magnitude, that divisor is 1e-20 or more.
Results may differ from a plain program's by a relative error of at most 0.024.
Values may be sent and summed in bfloat16 or wider, within the bound.
No kernel may reach another device: no remote copies, remote signals or barrier semaphores. Data moves between devices by JAX's collectives and lax.ppermute only.
A program may use at most 64 MiB of HBM per device.

v0:
```python
import jax
import jax.numpy as jnp
from jax import lax
from jax.sharding import PartitionSpec as P

TILE = 128
epsilon = 1e-06


def regroup(moved, senders, per_owner, block_rows, col_width):
    stacked = moved.reshape(senders, per_owner, block_rows, col_width)
    return jnp.swapaxes(stacked, 0, 1).reshape(senders * per_owner * block_rows, col_width)


def body(old_codes, old_scales, gate_pre, up_pre):
    n_fsdp = lax.axis_size("fsdp")
    n_tensor = lax.axis_size("tensor")
    f_index = lax.axis_index("fsdp")
    t_index = lax.axis_index("tensor")
    block_rows, full_width = old_codes.shape
    col_width = full_width // n_fsdp
    col_tiles = col_width // TILE
    per_owner = n_fsdp // n_tensor
    own_rows = block_rows * n_fsdp
    row_tiles = own_rows // TILE
    hidden = (jax.nn.silu(gate_pre.astype(jnp.float32)) * up_pre.astype(jnp.float32)).astype(
        jnp.bfloat16
    )
    sectioned = lax.all_to_all(old_codes, "fsdp", split_axis=1, concat_axis=0, tiled=True)
    scale_cols = lax.dynamic_slice_in_dim(old_scales, f_index * col_tiles, col_tiles, 1)
    moved = lax.all_to_all(
        sectioned.reshape(n_tensor, per_owner * block_rows, col_width),
        "tensor",
        split_axis=0,
        concat_axis=0,
        tiled=True,
    )
    final_rows = regroup(moved, n_tensor, per_owner, block_rows, col_width)
    scale_block = lax.dynamic_slice_in_dim(scale_cols, t_index * row_tiles, row_tiles, 0)
    tile_values = (
        final_rows.astype(jnp.float32).reshape(row_tiles, TILE, col_tiles, TILE)
        * scale_block[:, None, :, None]
    )
    new_scale = jnp.max(jnp.abs(tile_values), axis=(1, 3)) + epsilon
    new_codes = (tile_values / new_scale[:, None, :, None]).astype(jnp.bfloat16)
    weight = (
        (new_codes.astype(jnp.float32) * new_scale[:, None, :, None])
        .astype(jnp.bfloat16)
        .reshape(own_rows, col_width)
    )
    partial_value = jnp.dot(
        lax.all_gather(hidden, "fsdp", axis=0, tiled=True),
        weight,
        preferred_element_type=jnp.float32,
    )
    codes_t = new_codes.reshape(own_rows, col_width).T
    scales_t = new_scale.T
    mixed = lax.psum_scatter(
        partial_value.astype(jnp.bfloat16), "tensor", scatter_dimension=0, tiled=True
    )
    return (mixed, codes_t, scales_t)


def solution(mesh):
    return jax.shard_map(
        body,
        mesh=mesh,
        in_specs=(P(("fsdp", "tensor"), None), P(), P("fsdp", "tensor"), P("fsdp", "tensor")),
        out_specs=(P("tensor", "fsdp"), P("fsdp", "tensor"), P("fsdp", "tensor")),
        check_vma=False,
    )
```

profile of v0, /device:TPU:16, one launch (start us, length us, event | category | flops | bytes accessed | tf_op | source)
XLA Modules:
  0.0 263.3 jit_solution(17682116257781332109)
XLA Ops:
  7.2 0.0 all-gather.2.cloned.1.call-start
  7.2 1.8 fusion.7
  9.1 0.0 all-gather.2.cloned.1.call-update
  9.1 2.2 copy.20
  11.2 0.2 slice
  11.4 0.9 copy.14
  12.4 74.0 %all_to_all.21 = bf16[52,32,512]{2,0,1:T(8,128)(2,1)S(1)} all-to-all(bf16[52,32,512]{2,0,1:T(8,128)(2,1)S(1)} %copy.14), channel_id=1, replica_groups=mesh['fsdp'=32,'tensor'=16] {'fsdp'}, dimensions={1} | all-to-all | bytes 3407872 | tf_op jit(solution)/shard_map/all_to_all | solution.py:29
  86.4 1.3 reshape.38
  87.7 4.3 %all-to-all-start.1 = ((bf16[16,104,512]{2,1,0:T(8,128)(2,1)}), bf16[16,104,512]{2,1,0:T(8,128)(2,1)S(1)}, u32[]{:S(2)}, u32[]{:S(2)}) async-start(bf16[16,104,512]{2,1,0:T(8,128)(2,1)} %reshape.38), calls=%async_computation.1 | async-start | bytes 3407872 | tf_op jit(solution)/shard_map/all_to_all | solution.py:31
  92.0 0.2 reduce-scatter.2.cloned.1.call-start
  92.3 0.8 dynamic_slice.4
  93.1 33.8 %all-to-all-done.1 = bf16[16,104,512]{2,1,0:T(8,128)(2,1)S(1)} async-done(((bf16[16,104,512]{2,1,0:T(8,128)(2,1)}), bf16[16,104,512]{2,1,0:T(8,128)(2,1)S(1)}, u32[]{:S(2)}, u32[]{:S(2)}) %all-to-all-start.1) | async-done | bytes 1703968 | tf_op jit(solution)/shard_map/all_to_all | solution.py:31
  126.9 0.6 copy.15
  127.4 3.8 %copy.16 = f32[2,16,52,512]{3,2,1,0:T(8,128)} copy(f32[2,16,52,512]{3,1,2,0:T(8,128)S(1)} %bitcast.27) | data formatting | bytes 6815744 | tf_op jit(solution)/shard_map/convert_element_type | solution.py:41
  131.3 5.1 %reshape.40 = f32[13,128,4,128]{3,2,1,0:T(4,128)} reshape(f32[2,16,52,512]{3,2,1,0:T(8,128)} %copy.16) | data formatting | bytes 6815744 | tf_op jit(solution)/shard_map/convert_element_type | solution.py:41
  136.4 2.9 %reshape.39 = f32[1664,512]{1,0:T(8,128)S(1)} reshape(f32[2,16,52,512]{3,2,1,0:T(8,128)} %copy.16) | data formatting | bytes 6815744 | tf_op jit(solution)/shard_map/convert_element_type | solution.py:41
  139.3 3.0 %abs_reduce_fusion = f32[13,4]{1,0:T(8,128)S(1)} fusion(f32[13,128,4,128]{3,2,1,0:T(4,128)} %reshape.40, f32[13,4]{1,0:T(8,128)S(1)} %dynamic_slice.4), kind=kLoop, calls=%fused_computation.5 | loop fusion | flops 2555852 | bytes 3408288 | tf_op jit(solution)/shard_map/reduce_max | solution.py:44
  142.3 0.5 div.17
  142.8 0.0 copy-start
  142.8 0.5 mul.38
  143.4 1.3 copy-done
  144.6 2.5 fusion
  147.2 0.0 copy-start.1
  147.2 32.4 %all-gather.2.cloned.1.call-done = bf16[2048,1664]{1,0:T(8,128)(2,1)} async-done(((bf16[64,1664]{1,0:T(8,128)(2,1)}), bf16[2048,1664]{1,0:T(8,128)(2,1)}) %all-gather.2.cloned.1.call-update) | async-done | bytes 6815760 | tf_op jit(solution)/shard_map/all_gather | solution.py:52
  179.5 9.7 %convolution_convert_fusion = bf16[2048,512]{1,0:T(8,128)(2,1)} fusion(bf16[2048,1664]{1,0:T(8,128)(2,1)} %all-gather.2.cloned.1.call-done, bf16[1664,512]{1,0:T(8,128)(2,1)} %fusion, f32[208,8,4,128]{3,2,1,0:T(4,128)} %bitcast.29), kind=kOutput, calls=%fused_computation.6 | convolution fusion | flops 3493265408 | bytes 14024704 | tf_op jit(solution)/shard_map/dot_general | solution.py:51
  189.3 0.0 reduce-scatter.2.cloned.1.call-update
  189.3 0.0 copy-done.1
  189.3 2.3 copy.18
  191.6 0.7 copy.19
  192.3 64.2 %reduce-scatter.2.cloned.1.call-done = bf16[128,512]{1,0:T(8,128)(2,1)} async-done(((bf16[2048,512]{1,0:T(8,128)(2,1)}), bf16[128,512]{1,0:T(8,128)(2,1)}) %reduce-scatter.2.cloned.1.call-update) | async-done | bytes 131088 | tf_op jit(solution)/shard_map/reduce_scatter | solution.py:58
  (1 shorter events, 0.0 us)
Async XLA Ops:
  7.2 172.4 %all-gather.2.cloned.1.call-start = ((), (), s32[]{:S(2)}) async-start(), calls=%async_computation.3 | async-start | bytes 7028736 | tf_op jit(solution)/shard_map/all_gather | solution.py:52
  87.7 39.2 %all-to-all-start.1 = ((bf16[16,104,512]{2,1,0:T(8,128)(2,1)}), bf16[16,104,512]{2,1,0:T(8,128)(2,1)S(1)}, u32[]{:S(2)}, u32[]{:S(2)}) async-start(bf16[16,104,512]{2,1,0:T(8,128)(2,1)} %reshape.38), calls=%async_computation.1 | async-start | bytes 3407872 | tf_op jit(solution)/shard_map/all_to_all | solution.py:31
  92.0 164.5 %reduce-scatter.2.cloned.1.call-start = ((), (), s32[]{:S(2)}) async-start(), calls=%async_computation.4 | async-start | bytes 2228224 | tf_op jit(solution)/shard_map/reduce_scatter | solution.py:58
  142.8 1.8 copy-start
  147.2 42.1 %copy-start.1 = (bf16[1664,512]{1,0:T(8,128)(2,1)S(1)}, bf16[1664,512]{1,0:T(8,128)(2,1)}, u32[]{:S(2)}) copy-start(bf16[1664,512]{1,0:T(8,128)(2,1)} %fusion) | copy-start | bytes 5111812
Sparse Core Ops, SparseCore 0:
  11.2 168.3 all-gather.1
  189.4 67.0 reduce-scatter.1
where the time goes:
time: 264 us; the launch traced here: 263 us
  waiting for transfers between devices  130 us (49%)
  blocking collectives  74 us (28%)
  local copies, waits for them, and re-layouts  23.1 us (9%)
  between operations  14.1 us (5%)
  matrix products  9.71 us (4%)
  other arithmetic  7.42 us (3%)
  starting transfers between devices  4.58 us (2%)
    all_to_all x1, blocking collectives, body(): lax.all_to_all(old_codes, 'fsdp', split_axis=1, concat_axis=0, tiled=True)  74 us
    reduce_scatter x1, waiting for transfers between devices, body(): lax.psum_scatter(partial_value.astype(jnp.bfloat16), 'tensor', scatter_di...  64.2 us
    all_to_all x1, waiting for transfers between devices, body(): lax.all_to_all(sectioned.reshape(n_tensor, per_owner * block_rows, col_wi...  33.8 us
    all_gather x1, waiting for transfers between devices, body(): lax.all_gather(hidden, 'fsdp', axis=0, tiled=True)  32.4 us
    convert_element_type x4, local copies, waits for them, and re-layouts, body(): final_rows.astype(jnp.float32).reshape(row_tiles, TILE, col_tiles, TILE)  12.4 us
    dot_general x1, matrix products, body(): jnp.dot(lax.all_gather(hidden, 'fsdp', axis=0, tiled=True), weight, prefe...  9.71 us
    unnamed x7, local copies, waits for them, and re-layouts  6.44 us
  transfers between devices with their start and end apart: 3, of which 3 were waited for; matrix products, arithmetic and copies ran while one was open for 10% of the time, Pallas kernels for 0%

commit v1 on v0

--- a/solution.py
+++ b/solution.py
@@ -26,7 +26,9 @@
     hidden = (jax.nn.silu(gate_pre.astype(jnp.float32)) * up_pre.astype(jnp.float32)).astype(
         jnp.bfloat16
     )
-    sectioned = lax.all_to_all(old_codes, "fsdp", split_axis=1, concat_axis=0, tiled=True)
+    pieces = jnp.split(old_codes, lax.axis_size("fsdp"), axis=1)
+    received = lax.all_to_all(jnp.stack(pieces), "fsdp", 0, 0)
+    sectioned = jnp.concatenate(received, axis=0)
     scale_cols = lax.dynamic_slice_in_dim(old_scales, f_index * col_tiles, col_tiles, 1)
     moved = lax.all_to_all(
         sectioned.reshape(n_tensor, per_owner * block_rows, col_width),

time: 264 us -> 265 us (level)
  local copies, waits for them, and re-layouts: 23.1 us -> 28.8 us
    unnamed x7 -> x39, local copies, waits for them, and re-layouts: 6.44 us -> 13.2 us
    all_gather x1, waiting for transfers between devices: 32.4 us -> 26.6 us  [body(): lax.all_gather(hidden, 'fsdp', axis=0, tiled=True)]
    all_to_all x1, waiting for transfers between devices: 33.8 us -> 38.5 us  [body(): lax.all_to_all(sectioned.reshape(n_tensor, per_owner * block_rows, col_wi...]
  transfers between devices with their start and end apart: 3 -> 3, of which waited for: 3 -> 3; matrix products, arithmetic and copies ran while one was open for 10% -> 12% of each run, Pallas kernels for 0% -> 0%
where the time goes in v1:
time: 265 us; the launch traced here: 264 us
  waiting for transfers between devices  128 us (48%)
  blocking collectives  71.5 us (27%)
  local copies, waits for them, and re-layouts  28.8 us (11%)
  between operations  14.3 us (5%)
  matrix products  9.71 us (4%)
  other arithmetic  7.54 us (3%)
  starting transfers between devices  4.46 us (2%)
    all_to_all x1, blocking collectives, body(): received = lax.all_to_all(jnp.stack(pieces), 'fsdp', 0, 0)  71.5 us
    reduce_scatter x1, waiting for transfers between devices, body(): lax.psum_scatter(partial_value.astype(jnp.bfloat16), 'tensor', scatter_di...  63 us
    all_to_all x1, waiting for transfers between devices, body(): lax.all_to_all(sectioned.reshape(n_tensor, per_owner * block_rows, col_wi...  38.5 us
    all_gather x1, waiting for transfers between devices, body(): lax.all_gather(hidden, 'fsdp', axis=0, tiled=True)  26.6 us
    unnamed x39, local copies, waits for them, and re-layouts  13.2 us
    convert_element_type x4, local copies, waits for them, and re-layouts, body(): final_rows.astype(jnp.float32).reshape(row_tiles, TILE, col_tiles, TILE)  12.5 us
    dot_general x1, matrix products, body(): jnp.dot(lax.all_gather(hidden, 'fsdp', axis=0, tiled=True), weight, prefe...  9.71 us
  transfers between devices with their start and end apart: 3, of which 3 were waited for; matrix products, arithmetic and copies ran while one was open for 12% of the time, Pallas kernels for 0%

profile of v1, /device:TPU:16, one launch (start us, length us, event | category | flops | bytes accessed | tf_op | source)
XLA Modules:
  0.0 264.5 jit_solution(15389057564141532054)
XLA Ops:
  7.2 0.0 all-gather.2.cloned.1.call-start
  7.2 2.0 fusion.7
  9.2 0.8 constant_dynamic-update-slice_fusion.31
  10.0 0.8 constant_dynamic-update-slice_fusion.30
  10.9 0.8 constant_dynamic-update-slice_fusion.29
  11.7 0.8 constant_dynamic-update-slice_fusion.28
  12.5 0.8 constant_dynamic-update-slice_fusion.27
  13.3 0.8 constant_dynamic-update-slice_fusion.26
  14.2 0.8 constant_dynamic-update-slice_fusion.25
  15.0 0.8 constant_dynamic-update-slice_fusion.24
  15.8 0.8 constant_dynamic-update-slice_fusion.23
  16.9 71.5 %all_to_all.10 = bf16[32,52,512]{2,1,0:T(8,128)(2,1)S(1)} all-to-all(bf16[32,52,512]{2,1,0:T(8,128)(2,1)S(1)} %constant_dynamic-update-slice_fusion), channel_id=1, replica_groups=mesh['fsdp'=32,'tensor'=16] {'fsdp'}, dimensions={0} | all-to-all | bytes 3407872 | tf_op jit(solution)/shard_map/all_to_all | solution.py:30
  88.5 1.3 reshape_reshape.3
  89.8 4.4 %all-to-all-start.1 = ((bf16[16,104,512]{2,1,0:T(8,128)(2,1)}), bf16[16,104,512]{2,1,0:T(8,128)(2,1)S(1)}, u32[]{:S(2)}, u32[]{:S(2)}) async-start(bf16[16,104,512]{2,1,0:T(8,128)(2,1)} %reshape_reshape.3), calls=%async_computation.1 | async-start | bytes 3407872 | tf_op jit(solution)/shard_map/all_to_all | solution.py:33
  94.2 0.0 reduce-scatter.2.cloned.1.call-start
  94.2 0.8 dynamic_slice.4
  95.0 38.5 %all-to-all-done.1 = bf16[16,104,512]{2,1,0:T(8,128)(2,1)S(1)} async-done(((bf16[16,104,512]{2,1,0:T(8,128)(2,1)}), bf16[16,104,512]{2,1,0:T(8,128)(2,1)S(1)}, u32[]{:S(2)}, u32[]{:S(2)}) %all-to-all-start.1) | async-done | bytes 1703968 | tf_op jit(solution)/shard_map/all_to_all | solution.py:33
  133.6 0.6 copy.13
  134.1 3.8 %copy.14 = f32[2,16,52,512]{3,2,1,0:T(8,128)} copy(f32[2,16,52,512]{3,1,2,0:T(8,128)S(1)} %bitcast.87) | data formatting | bytes 6815744 | tf_op jit(solution)/shard_map/convert_element_type | solution.py:43
  138.0 5.2 %reshape.32 = f32[13,128,4,128]{3,2,1,0:T(4,128)} reshape(f32[2,16,52,512]{3,2,1,0:T(8,128)} %copy.14) | data formatting | bytes 6815744 | tf_op jit(solution)/shard_map/convert_element_type | solution.py:43
  143.1 2.9 %reshape.31 = f32[1664,512]{1,0:T(8,128)S(1)} reshape(f32[2,16,52,512]{3,2,1,0:T(8,128)} %copy.14) | data formatting | bytes 6815744 | tf_op jit(solution)/shard_map/convert_element_type | solution.py:43
  146.0 3.0 %abs_reduce_fusion = f32[13,4]{1,0:T(8,128)S(1)} fusion(f32[13,128,4,128]{3,2,1,0:T(4,128)} %reshape.32, f32[13,4]{1,0:T(8,128)S(1)} %dynamic_slice.4), kind=kLoop, calls=%fused_computation.5 | loop fusion | flops 2555852 | bytes 3408288 | tf_op jit(solution)/shard_map/reduce_max | solution.py:46
  149.1 0.5 div.17
  149.6 0.5 mul.38
  150.1 1.3 copy-done
  151.4 2.5 fusion
  153.9 26.6 %all-gather.2.cloned.1.call-done = bf16[2048,1664]{1,0:T(8,128)(2,1)} async-done(((bf16[64,1664]{1,0:T(8,128)(2,1)}), bf16[2048,1664]{1,0:T(8,128)(2,1)}) %all-gather.2.cloned.1.call-update) | async-done | bytes 6815760 | tf_op jit(solution)/shard_map/all_gather | solution.py:54
  180.5 9.7 %convolution_convert_fusion = bf16[2048,512]{1,0:T(8,128)(2,1)} fusion(bf16[2048,1664]{1,0:T(8,128)(2,1)} %all-gather.2.cloned.1.call-done, bf16[1664,512]{1,0:T(8,128)(2,1)} %fusion, f32[208,8,4,128]{3,2,1,0:T(4,128)} %bitcast.89), kind=kOutput, calls=%fused_computation.6 | convolution fusion | flops 3493265408 | bytes 14024704 | tf_op jit(solution)/shard_map/dot_general | solution.py:53
  190.3 1.4 copy-done.1
  191.7 2.3 copy.16
  194.0 0.7 copy.17
  194.7 63.0 %reduce-scatter.2.cloned.1.call-done = bf16[128,512]{1,0:T(8,128)(2,1)} async-done(((bf16[2048,512]{1,0:T(8,128)(2,1)}), bf16[128,512]{1,0:T(8,128)(2,1)}) %reduce-scatter.2.cloned.1.call-update) | async-done | bytes 131088 | tf_op jit(solution)/shard_map/reduce_scatter | solution.py:60
  (30 shorter events, 0.2 us)
Async XLA Ops:
  7.2 9.5 %copy-start.2 = (bf16[52,16384]{1,0:T(8,128)(2,1)S(1)}, bf16[52,16384]{1,0:T(8,128)(2,1)}, u32[]{:S(2)}) copy-start(bf16[52,16384]{1,0:T(8,128)(2,1)} %param.4) | copy-start | bytes 5111812
  7.2 173.3 %all-gather.2.cloned.1.call-start = ((), (), s32[]{:S(2)}) async-start(), calls=%async_computation.3 | async-start | bytes 7028736 | tf_op jit(solution)/shard_map/all_gather | solution.py:54
  89.8 43.8 %all-to-all-start.1 = ((bf16[16,104,512]{2,1,0:T(8,128)(2,1)}), bf16[16,104,512]{2,1,0:T(8,128)(2,1)S(1)}, u32[]{:S(2)}, u32[]{:S(2)}) async-start(bf16[16,104,512]{2,1,0:T(8,128)(2,1)} %reshape_reshape.3), calls=%async_computation.1 | async-start | bytes 3407872 | tf_op jit(solution)/shard_map/all_to_all | solution.py:33
  94.2 163.5 %reduce-scatter.2.cloned.1.call-start = ((), (), s32[]{:S(2)}) async-start(), calls=%async_computation.4 | async-start | bytes 2228224 | tf_op jit(solution)/shard_map/reduce_scatter | solution.py:60
  149.6 1.8 copy-start
  190.2 1.5 copy-start.1
Sparse Core Ops, SparseCore 0:
  11.2 169.3 all-gather.1
  190.4 67.2 reduce-scatter.1
